TPU v7x, 32 devices: a whole 2x2x4 slice. The times are simulated.
32 devices in a mesh: tm: 4 (over y, x), freq: 8 (over z, core).
Axes of the slice: x: 2, y: 2, z: 4, core: 2. Of those that a mesh axis runs over, the one named last changes fastest.
Arguments:
- records: bfloat16 [1024, 512, 512], P('freq', 'tm'), may hold values from -4 to 4
- gap_flags: int32 [1024, 16], P('freq', 'tm'), may hold values from -2147483648 to 2147483647
- station_mask: int32 [1024], P('freq'), may hold values 0 or 1
Outputs:
- cross_spectra: float32 [16, 2, 1024, 1024], P('freq', None, 'tm')
All inputs are finite; a program needn't handle non-finite values. No bound on the sum of `station_mask` on one device may be relied on, other than what follows from the above.
Results may differ from a plain program's by a relative error of at most 0.0013.
Values may be sent and summed in bfloat16 or wider, within the bound.
No kernel may reach another device: no remote copies, remote signals or barrier semaphores. Data moves between devices by JAX's collectives and lax.ppermute only.
A program may use at most 128 MiB of HBM per device.

v0:
```python
import math
import jax
import jax.numpy as jnp
from jax import lax
from jax.sharding import PartitionSpec as P

BAND_DEV = 2
FLOOR = 0.25


def transform_table(length, bin_count):
    sample_ids = jnp.arange(length, dtype=jnp.int32)
    bin_ids = jnp.arange(bin_count, dtype=jnp.int32)
    phase_ids = bin_ids[:, None] * sample_ids[None, :] % length
    angles = phase_ids.astype(jnp.float32) * (2.0 * math.pi / length)
    window_taper = 0.5 - 0.5 * jnp.cos(sample_ids.astype(jnp.float32) * (2.0 * math.pi / length))
    factor = window_taper / math.sqrt(length)
    dft_table = jnp.concatenate([jnp.cos(angles) * factor, -jnp.sin(angles) * factor], axis=0)
    return dft_table.astype(jnp.bfloat16)


def unpack_flags(packed_words):
    shifts = jnp.arange(32, dtype=jnp.int32)
    bit_values = jnp.bitwise_and(
        jnp.right_shift(packed_words[:, :, None], shifts[None, None, :]), 1
    )
    return bit_values.reshape(packed_words.shape[0], packed_words.shape[1] * 32)


def whiten(records, band_bins):
    bin_count = band_bins + 4
    dft_table = transform_table(records.shape[-1], bin_count)
    spectrum = jnp.einsum("cl,swl->scw", dft_table, records, preferred_element_type=jnp.float32)
    real_part = spectrum[:, :bin_count]
    imag_part = spectrum[:, bin_count:]
    magnitude = jnp.sqrt(real_part * real_part + imag_part * imag_part)
    smooth = (
        magnitude[:, 0:band_bins]
        + magnitude[:, 1 : band_bins + 1]
        + magnitude[:, 2 : band_bins + 2]
        + magnitude[:, 3 : band_bins + 3]
        + magnitude[:, 4 : band_bins + 4]
    ) / 5.0
    factor = 1.0 / jnp.maximum(smooth, FLOOR)
    whitened = jnp.stack(
        [real_part[:, 2 : band_bins + 2] * factor, imag_part[:, 2 : band_bins + 2] * factor], axis=2
    )
    return whitened.astype(jnp.bfloat16)


def block_terms(left_side, right_side):
    count_rows, bin_count, _, win_count = left_side.shape
    right_rows = right_side.shape[0]
    direct_left = left_side.reshape(count_rows, bin_count, 2 * win_count)
    turned_left = jnp.concatenate([left_side[:, :, 1], -left_side[:, :, 0]], axis=2)
    direct_right = right_side.reshape(right_rows, bin_count, 2 * win_count)
    real_part = jnp.einsum(
        "ifx,jfx->ifj", direct_left, direct_right, preferred_element_type=jnp.float32
    )
    imag_part = jnp.einsum(
        "ifx,jfx->ifj", turned_left, direct_right, preferred_element_type=jnp.float32
    )
    return jnp.stack([real_part, imag_part], axis=2).reshape(count_rows, 2 * bin_count, right_rows)


def local(records, gap_flags, station_mask):
    freq_size = lax.axis_size("freq")
    time_size = lax.axis_size("tm")
    band_bins = BAND_DEV * freq_size
    whitened = whiten(records, band_bins)
    kept_words = gap_flags * station_mask[:, None]
    spectra = lax.all_to_all(whitened, "freq", split_axis=1, concat_axis=0, tiled=True)
    all_words = lax.all_gather(kept_words, "freq", axis=0, tiled=True)
    here_flags = unpack_flags(all_words).astype(jnp.bfloat16)
    masked = spectra * here_flags[:, None, None, :]
    stations = spectra.shape[0]
    row_count = stations // time_size
    row_start = lax.axis_index("tm") * row_count
    every_words = lax.all_gather(all_words, "tm", axis=1, tiled=True)
    every_flags = unpack_flags(every_words).astype(jnp.bfloat16)
    row_flags = lax.dynamic_slice_in_dim(every_flags, row_start, row_count, 0)
    counts = jnp.dot(row_flags, every_flags.T, preferred_element_type=jnp.float32)
    window_part = lax.all_gather(masked, "tm", axis=3, tiled=True)
    left_side = lax.dynamic_slice_in_dim(window_part, row_start, row_count, 0)
    stacks = block_terms(left_side, window_part)
    divisor = jnp.maximum(counts, 1.0)
    result = stacks / divisor[:, None, :]
    return result.reshape(row_count, BAND_DEV, 2, stations).transpose(1, 2, 0, 3)


def solution(mesh):
    placed = (P("freq", "tm", None), P("freq", "tm"), P("freq"))
    return jax.shard_map(
        local, mesh=mesh, in_specs=placed, out_specs=P("freq", None, "tm", None), check_vma=False
    )
```

profile of v0, /device:TPU:0, one launch (start us, length us, event | category | flops | bytes accessed | tf_op | source)
XLA Modules:
  0.0 130.0 jit_solution(13890323300610356222)
XLA Ops:
  6.6 0.2 multiply_convert_fusion.1
  6.8 8.5 %convolution_bitcast_fusion = f32[128,40,128]{2,1,0:T(8,128)S(1)} fusion(bf16[128,128,512]{2,1,0:T(8,128)(2,1)} %param.3, bf16[20,512]{1,0:T(8,128)(2,1)S(1)} %get-tuple-element.10, bf16[20,512]{1,0:T(8,128)(2,1)S(1)} %get-tuple-element.9), kind=kOutput, calls=%fused_computation.5 | convolution fusion | flops 671170560 | bytes 19439616 | tf_op jit(solution)/shard_map/cl,swl->scw/dot_general | solution.py:33
  15.3 0.6 fusion.4
  15.9 0.7 fusion.13
  16.6 0.2 fusion.14
  16.8 0.1 pad_maximum_fusion
  16.9 0.0 copy-start.1
  16.9 0.0 copy-start.2
  16.9 1.2 copy.17
  18.2 6.3 %all-to-all-start = ((bf16[128,16,2,128]{3,0,2,1:T(8,128)(2,1)}), bf16[128,16,2,128]{3,0,2,1:T(8,128)(2,1)S(1)}, u32[]{:S(2)}, u32[]{:S(2)}) async-start(bf16[128,16,2,128]{3,0,2,1:T(8,128)(2,1)} %copy.17), calls=%async_computation | async-start | bytes 2097152 | tf_op jit(solution)/shard_map/all_to_all | solution.py:72
  24.5 0.0 all-gather.3.cloned.1.call-start
  24.6 0.1 shift_right_arithmetic.47
  24.7 0.0 copy-done.1
  24.7 0.0 copy-done.2
  24.7 32.5 %all_gather.9 = s32[1024,4]{0,1:T(4,128)S(1)} all-gather(s32[128,4]{0,1:T(4,128)S(1)} %broadcast_multiply_fusion), channel_id=1, replica_groups=mesh['tm'=4,'freq'=8] {'freq'}, dimensions={0}, use_global_device_ids=true | all-gather | bytes 18432 | tf_op jit(solution)/shard_map/all_gather | solution.py:73
  57.2 0.1 fusion.17
  57.3 0.2 copy.19
  57.5 0.0 all-to-all-done
  57.5 0.1 copy.18
  57.6 1.1 bitcast_multiply_fusion
  58.7 0.0 all-gather.3.cloned.1.call-update
  58.8 0.1 shift_right_arithmetic.53
  58.8 8.2 %all-gather = s32[4,4,1024]{2,1,0:T(4,128)S(1)} all-gather(s32[1,4,1024]{2,1,0:T(4,128)S(1)} %bitcast.60), channel_id=1, replica_groups=mesh['tm'=4,'freq'=8] {'tm'}, dimensions={0}, use_global_device_ids=true | all-gather | bytes 81920 | tf_op jit(solution)/shard_map/all_gather | solution.py:79
  67.1 0.3 fusion.2
  67.4 0.5 convolution_maximum_fusion
  67.9 0.3 copy.22
  68.2 41.3 %all-gather.3.cloned.1.call-done = bf16[1024,2,2,512]{3,0,1,2:T(8,128)(2,1)} async-done(((bf16[1024,2,2,128]{3,0,1,2:T(8,128)(2,1)}), bf16[1024,2,2,512]{3,0,1,2:T(8,128)(2,1)}) %all-gather.3.cloned.1.call-update) | async-done | bytes 4194320 | tf_op jit(solution)/shard_map/all_gather | solution.py:83
  109.5 0.0 copy-start
  109.5 1.4 %dynamic-slice_bitcast_fusion = bf16[2,2,32,8,512]{4,3,2,1,0:T(8,128)(2,1)S(1)} fusion(bf16[1024,2,2,512]{3,0,1,2:T(8,128)(2,1)} %all-gather.3.cloned.1.call-done, s32[]{:T(128)S(6)} %select_n.14), kind=kLoop, calls=%fused_computation.29 | loop fusion | bytes 2097156
  111.0 0.1 copy.25
  111.1 0.9 copy-done
  112.1 0.6 copy.24
  112.7 1.3 %convolution_bitcast_fusion.2 = f32[256,2,1,1024]{0,3,1,2:T(8,128)S(1)} fusion(bf16[1024,2,1024]{2,0,1:T(8,128)(2,1)S(1)} %bitcast.54, bf16[256,2,1024]{2,0,1:T(8,128)(2,1)S(1)} %bitcast.57), kind=kOutput, calls=%fused_computation.7 | convolution fusion | flops 1073741824 | bytes 7340032 | tf_op jit(solution)/shard_map/ifx,jfx->ifj/dot_general | solution.py:57
  114.0 0.1 dynamic-slice_bitcast_fusion.1
  114.1 1.3 %convolution_bitcast_fusion.1 = f32[256,2,1,1024]{0,3,1,2:T(8,128)S(1)} fusion(bf16[1024,2,1024]{2,0,1:T(8,128)(2,1)S(1)} %bitcast.55, bf16[256,2,512]{2,0,1:T(8,128)(2,1)S(1)} %get-tuple-element.8, bf16[256,2,512]{2,0,1:T(8,128)(2,1)S(1)} %get-tuple-element.7), kind=kOutput, calls=%fused_computation.6 | convolution fusion | flops 1075838976 | bytes 7340032 | tf_op jit(solution)/shard_map/ifx,jfx->ifj/dot_general | solution.py:60
  115.5 2.3 %fusion = f32[2,2,256,1024]{2,3,0,1:T(8,128)} fusion(f32[256,2,1,1024]{0,3,1,2:T(8,128)S(1)} %convolution_bitcast_fusion.1, f32[256,2,1,1024]{0,3,1,2:T(8,128)S(1)} %convolution_bitcast_fusion.2, f32[256,1024]{0,1:T(8,128)S(1)} %copy.22), kind=kLoop, calls=%fused_computation.1 | loop fusion | flops 2097152 | bytes 9437184 | tf_op jit(solution)/shard_map/transpose | solution.py:88
  117.8 5.3 %copy.23 = f32[2,2,256,1024]{3,2,1,0:T(8,128)} copy(f32[2,2,256,1024]{2,3,0,1:T(8,128)} %fusion) | data formatting | bytes 8388608 | tf_op jit(solution)/shard_map/transpose | solution.py:88
  (5 shorter events, 0.1 us)
Async XLA Ops:
  16.9 7.8 %copy-start.1 = (s32[128,4]{0,1:T(4,128)S(1)}, s32[128,4]{0,1:T(4,128)}, u32[]{:S(2)}) copy-start(s32[128,4]{0,1:T(4,128)} %param.4) | copy-start | bytes 6148
  16.9 7.7 %copy-start.2 = (s32[128]{0:T(128)S(1)}, s32[128]{0:T(128)}, u32[]{:S(2)}) copy-start(s32[128]{0:T(128)} %param.5) | copy-start | bytes 1540
  18.2 39.3 %all-to-all-start = ((bf16[128,16,2,128]{3,0,2,1:T(8,128)(2,1)}), bf16[128,16,2,128]{3,0,2,1:T(8,128)(2,1)S(1)}, u32[]{:S(2)}, u32[]{:S(2)}) async-start(bf16[128,16,2,128]{3,0,2,1:T(8,128)(2,1)} %copy.17), calls=%async_computation | async-start | bytes 2097152 | tf_op jit(solution)/shard_map/all_to_all | solution.py:72
  24.5 85.0 %all-gather.3.cloned.1.call-start = ((), (), s32[]{:S(2)}) async-start(), calls=%async_computation.1 | async-start | bytes 5242880 | tf_op jit(solution)/shard_map/all_gather | solution.py:83
  109.5 2.5 %copy-start = (bf16[1024,2,2,512]{3,0,1,2:T(8,128)(2,1)S(1)}, bf16[1024,2,2,512]{3,0,1,2:T(8,128)(2,1)}, u32[]{:S(2)}) copy-start(bf16[1024,2,2,512]{3,0,1,2:T(8,128)(2,1)} %all-gather.3.cloned.1.call-done) | copy-start | bytes 12582916
Sparse Core Ops, SparseCore 0:
  58.9 50.6 all-gather.2
where the time goes:
time: 130 us
  waiting for transfers between devices  41.3 us (32%)
  blocking collectives  40.7 us (31%)
  between operations  13.6 us (10%)
  matrix products  11.6 us (9%)
  local copies, waits for them, and re-layouts  10.5 us (8%)
  starting transfers between devices  6.38 us (5%)
  other arithmetic  5.85 us (4%)
    all_gather x1, waiting for transfers between devices, local(): window_part = lax.all_gather(masked, 'tm', axis=3, tiled=True)  41.3 us
    all_gather x1, blocking collectives, local(): all_words = lax.all_gather(kept_words, 'freq', axis=0, tiled=True)  32.5 us
    dot_general x1, matrix products, whiten(): jnp.einsum('cl,swl->scw', dft_table, records, preferred_element_type=jnp....  8.47 us
    all_gather x1, blocking collectives, local(): every_words = lax.all_gather(all_words, 'tm', axis=1, tiled=True)  8.24 us
    all_to_all x1, starting transfers between devices, local(): lax.all_to_all(whitened, 'freq', split_axis=1, concat_axis=0, tiled=True)  6.35 us
    transpose x1, local copies, waits for them, and re-layouts, local(): result.reshape(row_count, BAND_DEV, 2, stations).transpose(1, 2, 0, 3)  5.34 us
  transfers between devices with their start and end apart: 2, of which 1 were waited for; matrix products, arithmetic and copies ran while one was open for 1% of the time, Pallas kernels for 0%

commit v1 on v0

--- a/solution.py
+++ b/solution.py
@@ -70,7 +70,12 @@
     whitened = whiten(records, band_bins)
     kept_words = gap_flags * station_mask[:, None]
     spectra = lax.all_to_all(whitened, "freq", split_axis=1, concat_axis=0, tiled=True)
-    all_words = lax.all_gather(kept_words, "freq", axis=0, tiled=True)
+    ring = [kept_words]
+    for hop in range(7):
+        ring.append(lax.ppermute(ring[-1], "freq", [(dev, (dev + 1) % 8) for dev in range(8)]))
+    all_words = jnp.roll(
+        jnp.concatenate(ring[::-1], axis=0), (lax.axis_index("freq") + 1) * ring[0].shape[0], axis=0
+    )
     here_flags = unpack_flags(all_words).astype(jnp.bfloat16)
     masked = spectra * here_flags[:, None, None, :]
     stations = spectra.shape[0]

time: 130 us -> 148 us (1.14)
  waiting for transfers between devices: 41.3 us -> 90.7 us
  blocking collectives: 40.7 us -> 8.73 us
    all_gather x1 -> x0, blocking collectives: 32.5 us -> none  [local(): all_words = lax.all_gather(kept_words, 'freq', axis=0, tiled=True)]
    all_to_all x1, waiting for transfers between devices: 0.01 us -> 25.9 us  [local(): lax.all_to_all(whitened, 'freq', split_axis=1, concat_axis=0, tiled=True)]
    ppermute x0 -> x7, waiting for transfers between devices: none -> 22.7 us  [local(): lax.ppermute(ring[-1], 'freq', [(dev, (dev + 1) % 8) for dev in range(8)])]
    all_to_all x1, starting transfers between devices: 6.35 us -> 4.82 us  [local(): lax.all_to_all(whitened, 'freq', split_axis=1, concat_axis=0, tiled=True)]
  transfers between devices with their start and end apart: 2 -> 9, of which waited for: 1 -> 7; matrix products, arithmetic and copies ran while one was open for 1% -> 9% of each run, Pallas kernels for 0% -> 0%
where the time goes in v1:
time: 148 us; the launch traced here: 147 us
  waiting for transfers between devices  90.7 us (61%)
  between operations  13.7 us (9%)
  matrix products  11.6 us (8%)
  local copies, waits for them, and re-layouts  10.6 us (7%)
  blocking collectives  8.73 us (6%)
  other arithmetic  6.56 us (4%)
  starting transfers between devices  5.42 us (4%)
    all_gather x1, waiting for transfers between devices, local(): window_part = lax.all_gather(masked, 'tm', axis=3, tiled=True)  42.1 us
    all_to_all x1, waiting for transfers between devices, local(): lax.all_to_all(whitened, 'freq', split_axis=1, concat_axis=0, tiled=True)  25.9 us
    ppermute x7, waiting for transfers between devices, local(): lax.ppermute(ring[-1], 'freq', [(dev, (dev + 1) % 8) for dev in range(8)])  22.7 us
    all_gather x1, blocking collectives, local(): every_words = lax.all_gather(all_words, 'tm', axis=1, tiled=True)  8.73 us
    dot_general x1, matrix products, whiten(): jnp.einsum('cl,swl->scw', dft_table, records, preferred_element_type=jnp....  8.46 us
    transpose x1, local copies, waits for them, and re-layouts, local(): result.reshape(row_count, BAND_DEV, 2, stations).transpose(1, 2, 0, 3)  5.34 us
    all_to_all x1, starting transfers between devices, local(): lax.all_to_all(whitened, 'freq', split_axis=1, concat_axis=0, tiled=True)  4.82 us
  transfers between devices with their start and end apart: 9, of which 7 were waited for; matrix products, arithmetic and copies ran while one was open for 9% of the time, Pallas kernels for 0%

profile of v1, /device:TPU:0, one launch (start us, length us, event | category | flops | bytes accessed | tf_op | source)
XLA Modules:
  0.0 147.3 jit_solution(493992318661960791)
XLA Ops:
  6.5 0.7 broadcast_multiply_fusion
  7.2 0.5 collective-permute-start
  7.8 5.2 %collective-permute-done = s32[128,4]{0,1:T(4,128)S(1)} collective-permute-done((s32[128,4]{0,1:T(4,128)S(1)}, s32[128,4]{0,1:T(4,128)S(1)}, u32[]{:S(2)}, u32[]{:S(2)}) %collective-permute-start) | collective-permute-done | bytes 2080 | tf_op jit(solution)/shard_map/ppermute | solution.py:75
  13.0 0.0 collective-permute-start.1
  13.0 0.2 multiply_convert_fusion.1
  13.2 4.6 %collective-permute-done.1 = s32[128,4]{0,1:T(4,128)S(1)} collective-permute-done((s32[128,4]{0,1:T(4,128)S(1)}, s32[128,4]{0,1:T(4,128)S(1)}, u32[]{:S(2)}, u32[]{:S(2)}) %collective-permute-start.1) | collective-permute-done | bytes 2080 | tf_op jit(solution)/shard_map/ppermute | solution.py:75
  17.8 0.0 collective-permute-start.2
  17.8 8.5 %convolution_bitcast_fusion = f32[128,40,128]{2,1,0:T(8,128)S(1)} fusion(bf16[128,128,512]{2,1,0:T(8,128)(2,1)} %param.3, bf16[20,512]{1,0:T(8,128)(2,1)S(1)} %get-tuple-element.10, bf16[20,512]{1,0:T(8,128)(2,1)S(1)} %get-tuple-element.9), kind=kOutput, calls=%fused_computation.5 | convolution fusion | flops 671170560 | bytes 19439616 | tf_op jit(solution)/shard_map/cl,swl->scw/dot_general | solution.py:33
  26.3 0.0 collective-permute-done.2
  26.3 0.1 collective-permute-start.3
  26.4 0.6 fusion.4
  27.0 4.2 %collective-permute-done.3 = s32[128,4]{0,1:T(4,128)S(1)} collective-permute-done((s32[128,4]{0,1:T(4,128)S(1)}, s32[128,4]{0,1:T(4,128)S(1)}, u32[]{:S(2)}, u32[]{:S(2)}) %collective-permute-start.3) | collective-permute-done | bytes 2080 | tf_op jit(solution)/shard_map/ppermute | solution.py:75
  31.2 0.0 collective-permute-start.4
  31.2 0.7 fusion.13
  31.9 4.1 %collective-permute-done.4 = s32[128,4]{0,1:T(4,128)S(1)} collective-permute-done((s32[128,4]{0,1:T(4,128)S(1)}, s32[128,4]{0,1:T(4,128)S(1)}, u32[]{:S(2)}, u32[]{:S(2)}) %collective-permute-start.4) | collective-permute-done | bytes 2080 | tf_op jit(solution)/shard_map/ppermute | solution.py:75
  36.0 0.0 collective-permute-start.5
  36.0 0.2 fusion.14
  36.2 4.6 %collective-permute-done.5 = s32[128,4]{0,1:T(4,128)S(1)} collective-permute-done((s32[128,4]{0,1:T(4,128)S(1)}, s32[128,4]{0,1:T(4,128)S(1)}, u32[]{:S(2)}, u32[]{:S(2)}) %collective-permute-start.5) | collective-permute-done | bytes 2080 | tf_op jit(solution)/shard_map/ppermute | solution.py:75
  40.8 0.0 collective-permute-start.6
  40.8 0.1 pad_maximum_fusion
  40.9 0.0 copy-start.1
  40.9 0.0 copy-start.2
  40.9 1.2 copy.17
  42.2 4.8 %all-to-all-start = ((bf16[128,16,2,128]{3,0,2,1:T(8,128)(2,1)}), bf16[128,16,2,128]{3,0,2,1:T(8,128)(2,1)S(1)}, u32[]{:S(2)}, u32[]{:S(2)}) async-start(bf16[128,16,2,128]{3,0,2,1:T(8,128)(2,1)} %copy.17), calls=%async_computation | async-start | bytes 2097152 | tf_op jit(solution)/shard_map/all_to_all | solution.py:72
  47.0 0.0 all-gather.3.cloned.1.call-start
  47.0 0.1 shift_right_arithmetic.47
  47.1 0.0 collective-permute-done.6
  47.2 0.0 copy-done.1
  47.2 0.0 copy-done.2
  47.4 0.1 fusion.17
  47.5 0.2 copy.19
  47.7 25.9 %all-to-all-done = bf16[128,16,2,128]{3,0,2,1:T(8,128)(2,1)S(1)} async-done(((bf16[128,16,2,128]{3,0,2,1:T(8,128)(2,1)}), bf16[128,16,2,128]{3,0,2,1:T(8,128)(2,1)S(1)}, u32[]{:S(2)}, u32[]{:S(2)}) %all-to-all-start) | async-done | bytes 1048608 | tf_op jit(solution)/shard_map/all_to_all | solution.py:72
  73.5 0.1 copy.18
  73.6 1.1 bitcast_multiply_fusion
  74.7 0.0 all-gather.3.cloned.1.call-update
  74.8 0.1 shift_right_arithmetic.53
  74.9 8.7 %all-gather = s32[4,4,1024]{2,1,0:T(4,128)S(1)} all-gather(s32[1,4,1024]{2,1,0:T(4,128)S(1)} %fusion.36), channel_id=1, replica_groups=mesh['tm'=4,'freq'=8] {'tm'}, dimensions={0}, use_global_device_ids=true | all-gather | bytes 81920 | tf_op jit(solution)/shard_map/all_gather | solution.py:84
  83.6 0.3 fusion.2
  83.9 0.5 convolution_maximum_fusion
  84.4 0.3 copy.22
  84.8 42.1 %all-gather.3.cloned.1.call-done = bf16[1024,2,2,512]{3,0,1,2:T(8,128)(2,1)} async-done(((bf16[1024,2,2,128]{3,0,1,2:T(8,128)(2,1)}), bf16[1024,2,2,512]{3,0,1,2:T(8,128)(2,1)}) %all-gather.3.cloned.1.call-update) | async-done | bytes 4194320 | tf_op jit(solution)/shard_map/all_gather | solution.py:88
  126.8 0.0 copy-start
  126.9 1.4 dynamic-slice_bitcast_fusion
  128.3 0.1 copy.25
  128.4 0.9 copy-done
  129.4 0.6 copy.24
  130.0 1.3 convolution_bitcast_fusion.2
  131.3 0.1 dynamic-slice_bitcast_fusion.1
  131.4 1.3 convolution_bitcast_fusion.1
  132.8 2.3 %fusion = f32[2,2,256,1024]{2,3,0,1:T(8,128)} fusion(f32[256,2,1,1024]{0,3,1,2:T(8,128)S(1)} %convolution_bitcast_fusion.1, f32[256,2,1,1024]{0,3,1,2:T(8,128)S(1)} %convolution_bitcast_fusion.2, f32[256,1024]{0,1:T(8,128)S(1)} %copy.22), kind=kLoop, calls=%fused_computation.1 | loop fusion | flops 2097152 | bytes 9437184 | tf_op jit(solution)/shard_map/transpose | solution.py:93
  135.1 5.3 %copy.23 = f32[2,2,256,1024]{3,2,1,0:T(8,128)} copy(f32[2,2,256,1024]{2,3,0,1:T(8,128)} %fusion) | data formatting | bytes 8388608 | tf_op jit(solution)/shard_map/transpose | solution.py:93
  (22 shorter events, 0.2 us)
Async XLA Ops:
  7.2 5.8 %collective-permute-start = (s32[128,4]{0,1:T(4,128)S(1)}, s32[128,4]{0,1:T(4,128)S(1)}, u32[]{:S(2)}, u32[]{:S(2)}) collective-permute-start(s32[128,4]{0,1:T(4,128)S(1)} %broadcast_multiply_fusion), channel_id=1, source_target_pairs={{0,1},{1,2},{2,3},{3,4},{4,5},{5,6},{6,7},{7,0},{8,9},{9,10},{10,1... | collective-permute-start | bytes 6152 | tf_op jit(solution)/shard_map/ppermute | solution.py:75
  13.0 4.8 %collective-permute-start.1 = (s32[128,4]{0,1:T(4,128)S(1)}, s32[128,4]{0,1:T(4,128)S(1)}, u32[]{:S(2)}, u32[]{:S(2)}) collective-permute-start(s32[128,4]{0,1:T(4,128)S(1)} %collective-permute-done), channel_id=1, source_target_pairs={{0,1},{1,2},{2,3},{3,4},{4,5},{5,6},{6,7},{7,0},{8,9},{9,10},{10,1... | collective-permute-start | bytes 6152 | tf_op jit(solution)/shard_map/ppermute | solution.py:75
  17.8 8.5 %collective-permute-start.2 = (s32[128,4]{0,1:T(4,128)S(1)}, s32[128,4]{0,1:T(4,128)S(1)}, u32[]{:S(2)}, u32[]{:S(2)}) collective-permute-start(s32[128,4]{0,1:T(4,128)S(1)} %collective-permute-done.1), channel_id=1, source_target_pairs={{0,1},{1,2},{2,3},{3,4},{4,5},{5,6},{6,7},{7,0},{8,9},{9,10},{10,1... | collective-permute-start | bytes 6152 | tf_op jit(solution)/shard_map/ppermute | solution.py:75
  26.3 4.9 %collective-permute-start.3 = (s32[128,4]{0,1:T(4,128)S(1)}, s32[128,4]{0,1:T(4,128)S(1)}, u32[]{:S(2)}, u32[]{:S(2)}) collective-permute-start(s32[128,4]{0,1:T(4,128)S(1)} %collective-permute-done.2), channel_id=1, source_target_pairs={{0,1},{1,2},{2,3},{3,4},{4,5},{5,6},{6,7},{7,0},{8,9},{9,10},{10,1... | collective-permute-start | bytes 6152 | tf_op jit(solution)/shard_map/ppermute | solution.py:75
  31.2 4.8 %collective-permute-start.4 = (s32[128,4]{0,1:T(4,128)S(1)}, s32[128,4]{0,1:T(4,128)S(1)}, u32[]{:S(2)}, u32[]{:S(2)}) collective-permute-start(s32[128,4]{0,1:T(4,128)S(1)} %collective-permute-done.3), channel_id=1, source_target_pairs={{0,1},{1,2},{2,3},{3,4},{4,5},{5,6},{6,7},{7,0},{8,9},{9,10},{10,1... | collective-permute-start | bytes 6152 | tf_op jit(solution)/shard_map/ppermute | solution.py:75
  36.0 4.8 %collective-permute-start.5 = (s32[128,4]{0,1:T(4,128)S(1)}, s32[128,4]{0,1:T(4,128)S(1)}, u32[]{:S(2)}, u32[]{:S(2)}) collective-permute-start(s32[128,4]{0,1:T(4,128)S(1)} %collective-permute-done.4), channel_id=1, source_target_pairs={{0,1},{1,2},{2,3},{3,4},{4,5},{5,6},{6,7},{7,0},{8,9},{9,10},{10,1... | collective-permute-start | bytes 6152 | tf_op jit(solution)/shard_map/ppermute | solution.py:75
  40.8 6.3 %collective-permute-start.6 = (s32[128,4]{0,1:T(4,128)S(1)}, s32[128,4]{0,1:T(4,128)S(1)}, u32[]{:S(2)}, u32[]{:S(2)}) collective-permute-start(s32[128,4]{0,1:T(4,128)S(1)} %collective-permute-done.5), channel_id=1, source_target_pairs={{0,1},{1,2},{2,3},{3,4},{4,5},{5,6},{6,7},{7,0},{8,9},{9,10},{10,1... | collective-permute-start | bytes 6152 | tf_op jit(solution)/shard_map/ppermute | solution.py:75
  40.9 6.3 %copy-start.1 = (s32[128,4]{0,1:T(4,128)S(1)}, s32[128,4]{0,1:T(4,128)}, u32[]{:S(2)}) copy-start(s32[128,4]{0,1:T(4,128)} %param.4) | copy-start | bytes 6148
  40.9 6.3 %copy-start.2 = (s32[128]{0:T(128)S(1)}, s32[128]{0:T(128)}, u32[]{:S(2)}) copy-start(s32[128]{0:T(128)} %param.5) | copy-start | bytes 1540
  42.2 31.4 %all-to-all-start = ((bf16[128,16,2,128]{3,0,2,1:T(8,128)(2,1)}), bf16[128,16,2,128]{3,0,2,1:T(8,128)(2,1)S(1)}, u32[]{:S(2)}, u32[]{:S(2)}) async-start(bf16[128,16,2,128]{3,0,2,1:T(8,128)(2,1)} %copy.17), calls=%async_computation | async-start | bytes 2097152 | tf_op jit(solution)/shard_map/all_to_all | solution.py:72
  47.0 79.9 %all-gather.3.cloned.1.call-start = ((), (), s32[]{:S(2)}) async-start(), calls=%async_computation.1 | async-start | bytes 5242880 | tf_op jit(solution)/shard_map/all_gather | solution.py:88
  126.8 2.5 %copy-start = (bf16[1024,2,2,512]{3,0,1,2:T(8,128)(2,1)S(1)}, bf16[1024,2,2,512]{3,0,1,2:T(8,128)(2,1)}, u32[]{:S(2)}) copy-start(bf16[1024,2,2,512]{3,0,1,2:T(8,128)(2,1)} %all-gather.3.cloned.1.call-done) | copy-start | bytes 12582916
Sparse Core Ops, SparseCore 0:
  74.9 51.9 all-gather.2
